TPU v7x, 32 devices: a whole 2x2x4 slice. The times are simulated.
32 devices in a mesh: pen: 16 (over z, x, core), coil: 2 (over y).
Axes of the slice: x: 2, y: 2, z: 4, core: 2. Of those that a mesh axis runs over, the one named last changes fastest.
Arguments:
- image_field: float32 [512, 512, 2, 128], P('pen'), may hold values from -6 to 6
- coil_maps: bfloat16 [2, 512, 512, 2, 128], P('coil', 'pen'), may hold values from -5 to 5
- samples: bfloat16 [2, 4096, 128, 2, 128], P('coil', 'pen'), may hold values from -6 to 6
- kernels: bfloat16 [4096, 128, 128], P('pen'), may hold values from -0.5 to 0.5
- tile_of_block: int32 [4096], P('pen'), may hold values from 0 to 2047, as said below
Outputs:
- gradient: float32 [512, 512, 2, 128], P('pen', 'coil')
Inputs may be any that keep to these rules, and one draw needn't show every extreme that they name: The tile of every block lies with the block: tile_of_block[b] // 128 == b // 256; every tile is named by at least one block.
All inputs are finite; a program needn't handle non-finite values.
Results may differ from a plain program's by a relative error of at most 0.012.
Values may be sent and summed in bfloat16 or wider, within the bound.
No kernel may reach another device: no remote copies, remote signals or barrier semaphores. Data moves between devices by JAX's collectives and lax.ppermute only.
A program may use at most 256 MiB of HBM per device.

v0:
```python
import math
import jax
import jax.numpy as jnp
from jax import lax
from jax.sharding import PartitionSpec as P

NL = 512
NZ = 128
TILE = 128
tv_weight = 2.0


def shifted(shard, axis, by):
    length = lax.axis_size(axis)
    pairs = [(i, i + by) for i in range(length) if 0 <= i + by < length]
    return lax.ppermute(shard, axis, pairs)


def dft_tables(length, direction):
    index = lax.iota(jnp.int32, length)
    phase = index[:, None] * index[None, :] % length
    angle = 2.0 * math.pi / length * phase.astype(jnp.float32)
    cosine = jnp.cos(angle) / math.sqrt(length)
    sine = direction * jnp.sin(angle) / math.sqrt(length)
    table = jnp.stack([jnp.stack([cosine, sine], -1), jnp.stack([-sine, cosine], -1)], 1)
    high_part = table.astype(jnp.bfloat16)
    low_part = (table - high_part.astype(jnp.float32)).astype(jnp.bfloat16)
    return (high_part, low_part)


def along_second(tables, values):
    first = jnp.einsum("kpxr,yxrz->ykpz", tables[0], values, preferred_element_type=jnp.float32)
    return first + jnp.einsum(
        "kpxr,yxrz->ykpz", tables[1], values, preferred_element_type=jnp.float32
    )


def along_first(tables, values):
    first = jnp.einsum("kpyr,yxrz->kxpz", tables[0], values, preferred_element_type=jnp.float32)
    return first + jnp.einsum(
        "kpyr,yxrz->kxpz", tables[1], values, preferred_element_type=jnp.float32
    )


def flux_fields(extended, first_row, first_col):
    center = extended[:-1, :-1]
    row_ids = first_row + jnp.arange(center.shape[0])
    col_ids = first_col + jnp.arange(center.shape[1])
    diff_y = (extended[1:, :-1] - center) * (row_ids != NL - 1)[:, None, None, None]
    diff_x = (extended[:-1, 1:] - center) * (col_ids != NL - 1)[None, :, None, None]
    diff_z = jnp.concatenate(
        [center[..., 1:] - center[..., :-1], jnp.zeros_like(center[..., :1])], 3
    )
    norm_den = jnp.sqrt(
        1.0 + jnp.sum(diff_y * diff_y + diff_x * diff_x + diff_z * diff_z, axis=2, keepdims=True)
    )
    inside = ((row_ids >= 0)[:, None] & (col_ids >= 0)[None, :]).astype(jnp.float32)[
        :, :, None, None
    ]
    return (diff_y / norm_den * inside, diff_x / norm_den * inside, diff_z / norm_den * inside)


def plane_divergence(flux_z):
    return jnp.concatenate([jnp.zeros_like(flux_z[..., :1]), flux_z[..., :-1]], 3) - flux_z


def on_device(image_field, coil_maps, samples, kernels, tile_of_block):
    own_rows = image_field.shape[0]
    pen_count = lax.axis_size("pen")
    half_cols = NL // lax.axis_size("coil")
    local_cols = NL // pen_count
    pen_id = lax.axis_index("pen")
    coil_id = lax.axis_index("coil")
    row_start = pen_id * own_rows
    col_start = coil_id * half_cols
    map_real = coil_maps[0, :, :, 0].astype(jnp.float32)
    map_imag = coil_maps[0, :, :, 1].astype(jnp.float32)
    field_real = image_field[:, :, 0]
    field_imag = image_field[:, :, 1]
    coil_image = jnp.stack(
        [
            map_real * field_real - map_imag * field_imag,
            map_real * field_imag + map_imag * field_real,
        ],
        2,
    ).astype(jnp.bfloat16)
    forward_tab = dft_tables(NL, 1.0)
    adjoint_tab = dft_tables(NL, -1.0)
    rows_spectrum = along_second(forward_tab, coil_image).astype(jnp.bfloat16)
    kspace_grid = along_first(
        forward_tab, lax.all_to_all(rows_spectrum, "pen", split_axis=1, concat_axis=0, tiled=True)
    ).astype(jnp.bfloat16)
    grid_tiles = (
        kspace_grid.reshape(NL // TILE, TILE, local_cols, 2 * NZ)
        .transpose(2, 0, 1, 3)
        .reshape(-1, TILE, 2 * NZ)
    )
    tile_count = grid_tiles.shape[0]
    local_ids = tile_of_block - pen_id * tile_count
    picked = jnp.take(grid_tiles, local_ids, axis=0)
    predicted = jnp.einsum("bst,btc->bsc", kernels, picked, preferred_element_type=jnp.float32)
    measured = samples[0].reshape(predicted.shape).astype(jnp.float32)
    misfit = (predicted - measured).astype(jnp.bfloat16)
    back_terms = jnp.einsum("bst,bsc->btc", kernels, misfit, preferred_element_type=jnp.float32)
    onehot = (local_ids[:, None] == jnp.arange(tile_count, dtype=jnp.int32)[None, :]).astype(
        jnp.float32
    )
    back_tiles = jnp.einsum(
        "bl,btc->ltc", onehot, back_terms, precision=lax.Precision.HIGHEST
    ).astype(jnp.bfloat16)
    back_grid = (
        back_tiles.reshape(local_cols, NL // TILE, TILE, 2 * NZ)
        .transpose(1, 2, 0, 3)
        .reshape(NL, local_cols, 2, NZ)
    )
    back_rows = along_first(adjoint_tab, back_grid).astype(jnp.bfloat16)
    back_image = along_second(
        adjoint_tab, lax.all_to_all(back_rows, "pen", split_axis=0, concat_axis=1, tiled=True)
    )
    back_real = back_image[:, :, 0]
    back_imag = back_image[:, :, 1]
    coil_term = jnp.stack(
        [map_real * back_real + map_imag * back_imag, map_real * back_imag - map_imag * back_real],
        2,
    )
    summed = lax.psum(coil_term, "coil")
    data_gradient = lax.dynamic_slice_in_dim(summed, col_start, half_cols, 1)
    padded = jnp.pad(image_field, ((0, 0), (1, 1), (0, 0), (0, 0)))
    window = lax.dynamic_slice_in_dim(padded, col_start, half_cols + 2, 1)
    upper_row = shifted(window[:1], "pen", -1)
    extended = jnp.concatenate([window, upper_row], 0)
    flux_y, flux_x, flux_z = flux_fields(extended, row_start, col_start - 1)
    lower_row = shifted(flux_y[-1:], "pen", 1)
    flux_before = jnp.concatenate([lower_row, flux_y[:-1]], 0)
    tv_part = (
        flux_before[:, 1:]
        - flux_y[:, 1:]
        + flux_x[:, :-1]
        - flux_x[:, 1:]
        + plane_divergence(flux_z[:, 1:])
    )
    return data_gradient + tv_weight * tv_part


def solution(mesh):
    in_specs = (
        P("pen", None, None, None),
        P("coil", "pen", None, None, None),
        P("coil", "pen", None, None, None),
        P("pen", None, None),
        P("pen"),
    )
    out_specs = P("pen", "coil", None, None)
    return jax.shard_map(
        on_device, mesh=mesh, in_specs=in_specs, out_specs=out_specs, check_vma=False
    )
```

profile of v0, /device:TPU:0, one launch (start us, length us, event | category | flops | bytes accessed | tf_op | source)
XLA Modules:
  0.0 1350.3 jit_solution(1019381093489078857)
XLA Ops:
  20.2 25.0 %copy.32 = f32[32,512,2,128]{1,3,2,0:T(8,128)} copy(f32[32,512,2,128]{3,2,1,0:T(2,128)} %param.5) | data formatting | bytes 33554432 | tf_op args[0]
  45.2 17.5 %fusion.90 = (bf16[1,32,512,1,128]{4,3,2,1,0:T(2,128)(2,1)}, bf16[1,32,512,1,128]{4,3,2,1,0:T(2,128)(2,1)}) fusion(bf16[1,32,512,2,128]{4,3,2,1,0:T(2,128)(2,1)} %param.6), kind=kLoop, calls=%fused_computation.127 | loop fusion | bytes 16777216 | tf_op jit(solution)/shard_map/slice | solution.py:76
  62.7 18.3 %copy.75 = bf16[1,32,512,1,128]{2,4,1,3,0:T(8,128)(2,1)} copy(bf16[1,32,512,1,128]{4,3,2,1,0:T(2,128)(2,1)} %get-tuple-element.13) | data formatting | bytes 8388608
  81.0 18.3 %copy.76 = bf16[1,32,512,1,128]{2,4,1,3,0:T(8,128)(2,1)} copy(bf16[1,32,512,1,128]{4,3,2,1,0:T(2,128)(2,1)} %get-tuple-element.14) | data formatting | bytes 8388608
  126.7 17.4 %fusion.37 = bf16[32,512,2,128]{1,3,2,0:T(8,128)(2,1)} fusion(bf16[32,512,1,128]{1,3,2,0:T(8,128)(2,1)} %copy-done.4, bf16[32,512,1,128]{1,3,2,0:T(8,128)(2,1)} %copy-done.3, f32[32,128,512,2,1]{2,1,4,3,0:T(8,128)} %fusion.36, f32[512,1,512,2]{2,0,3,1:T(8,128)} %copy-done.8, f32[512,1,512,2]{2,0,3,1:T(8,128)} %copy-done.10), kind=kOutput, calls=%fused_computation.63 | convolution fusion | flops 8620343296 | bytes 37748736 | tf_op jit(solution)/shard_map/kpxr,yxrz->ykpz/dot_general | solution.py:33
  144.1 21.3 %copy.35 = bf16[32,512,2,128]{3,2,0,1:T(2,128)(2,1)} copy(bf16[32,512,2,128]{1,3,2,0:T(8,128)(2,1)} %fusion.37) | data formatting | bytes 16777216 | tf_op jit(solution)/shard_map/convert_element_type | solution.py:89
  172.9 45.1 %copy.42 = f32[1,256,128,2,128]{2,4,3,1,0:T(8,128)} copy(bf16[1,256,128,2,128]{4,3,2,1,0:T(2,128)(2,1)} %param.7) | data formatting | bytes 50331648 | tf_op jit(solution)/shard_map/convert_element_type | solution.py:102
  218.0 105.4 %all-to-all-done = bf16[32,512,2,128]{3,2,0,1:T(2,128)(2,1)} async-done(((bf16[32,512,2,128]{3,2,0,1:T(2,128)(2,1)}), bf16[32,512,2,128]{3,2,0,1:T(2,128)(2,1)}, u32[]{:S(2)}, u32[]{:S(2)}) %all-to-all-start) | async-done | bytes 8388640 | tf_op jit(solution)/shard_map/all_to_all | solution.py:91
  323.4 16.5 %copy.36 = bf16[32,512,2,128]{3,1,2,0:T(8,128)(2,1)} copy(bf16[32,512,2,128]{3,2,0,1:T(2,128)(2,1)} %all-to-all-done) | data formatting | bytes 16777216 | tf_op jit(solution)/shard_map/all_to_all | solution.py:91
  349.2 14.0 %copy.55 = bf16[512,32,2,128,1]{0,3,2,4,1:T(8,128)(2,1)} copy(bf16[512,32,2,128,1]{3,1,2,0,4:T(8,128)(2,1)} %bitcast.154) | data formatting | bytes 16777216 | tf_op jit(solution)/shard_map/all_to_all | solution.py:91
  363.2 16.4 %fusion.68 = f32[32,128,512,2,1]{2,1,4,3,0:T(8,128)} fusion(bf16[512,32,2,128,1]{0,3,2,4,1:T(8,128)(2,1)} %copy.55, f32[512,1,512,2]{2,0,3,1:T(8,128)S(1)} %copy-done.9, f32[512,1,512,2]{2,0,3,1:T(8,128)} %copy-done.10), kind=kOutput, calls=%fused_computation.100 | convolution fusion | flops 8594128896 | bytes 29360128 | tf_op jit(solution)/shard_map/kpyr,yxrz->kxpz/dot_general | solution.py:39
  379.7 17.1 %fusion.38 = bf16[512,32,2,128]{0,3,2,1:T(8,128)(2,1)} fusion(bf16[512,32,2,128,1]{0,3,2,4,1:T(8,128)(2,1)} %copy.55, f32[32,128,512,2,1]{2,1,4,3,0:T(8,128)} %fusion.68, f32[512,1,512,2]{2,0,3,1:T(8,128)S(1)} %copy-done.9, f32[512,1,512,2]{2,0,3,1:T(8,128)S(1)} %copy-done.11), kind=kOutput, calls=%fused_computation.64 | convolution fusion | flops 8603566080 | bytes 37748736 | tf_op jit(solution)/shard_map/kpyr,yxrz->kxpz/dot_general | solution.py:40
  409.2 13.3 copy.40
  422.5 13.2 gather_fusion
  435.7 38.4 %fusion.10 = f32[256,128,256]{1,2,0:T(8,128)} fusion(bf16[256,128,128]{2,1,0:T(8,128)(2,1)} %param.8, f32[256,128,256]{1,2,0:T(8,128)} %bitcast.151, bf16[256,128,256]{2,1,0:T(8,128)(2,1)} %gather_fusion, pred[256]{0:T(512)(128)(4,1)S(1)} %get-tuple-element.5), kind=kOutput, calls=%fused_computation.30 | convolution fusion | flops 4320133120 | bytes 92274944 | tf_op jit(solution)/shard_map/bst,bsc->btc/dot_general | solution.py:104
  474.1 33.4 %copy.43 = f32[256,128,256]{2,0,1:T(8,128)} copy(f32[256,128,256]{1,2,0:T(8,128)} %fusion.10) | data formatting | bytes 67108864 | tf_op jit(solution)/shard_map/bst,bsc->btc/dot_general | solution.py:104
  507.5 20.8 %convolution_convert_fusion = bf16[128,128,256]{2,0,1:T(8,128)(2,1)} fusion(f32[256,128,256]{2,0,1:T(8,128)} %copy.43, s32[256]{0:T(256)S(1)} %get-tuple-element.6), kind=kOutput, calls=%fused_computation.60 | convolution fusion | flops 12889128960 | bytes 41944064 | tf_op jit(solution)/shard_map/bl,btc->ltc/dot_general | solution.py:108
  540.8 18.0 %copy.44 = bf16[4,128,32,256]{1,0,3,2:T(4,128)(2,1)} copy(bf16[4,128,32,256]{3,0,2,1:T(4,128)(2,1)} %bitcast.155) | data formatting | bytes 16777216 | tf_op jit(solution)/shard_map/transpose | solution.py:113
  558.8 13.2 reshape.238
  572.1 16.8 %fusion.32 = f32[32,128,512,2,1]{2,1,4,3,0:T(8,128)} fusion(bf16[512,32,2,128,1]{0,3,2,1,4:T(8,128)(2,1)} %reshape.238, f32[512,1,512,2]{2,0,3,1:T(8,128)} %get-tuple-element.17, f32[512,1,512,2]{2,0,3,1:T(8,128)S(1)} %copy-done.5), kind=kOutput, calls=%fused_computation.57 | convolution fusion | flops 8594128896 | bytes 29360128 | tf_op jit(solution)/shard_map/kpyr,yxrz->kxpz/dot_general | solution.py:39
  588.9 16.9 %fusion.39 = bf16[512,32,2,128]{0,3,2,1:T(8,128)(2,1)} fusion(bf16[512,32,2,128,1]{0,3,2,1,4:T(8,128)(2,1)} %reshape.238, f32[32,128,512,2,1]{2,1,4,3,0:T(8,128)} %fusion.32, f32[512,1,512,2]{2,0,3,1:T(8,128)S(1)} %copy-done.6, f32[512,1,512,2]{2,0,3,1:T(8,128)S(1)} %copy-done.5), kind=kOutput, calls=%fused_computation.65 | convolution fusion | flops 8603566080 | bytes 37748736 | tf_op jit(solution)/shard_map/kpyr,yxrz->kxpz/dot_general | solution.py:40
  605.8 21.2 %copy.45 = bf16[512,32,2,128]{3,2,1,0:T(2,128)(2,1)} copy(bf16[512,32,2,128]{0,3,2,1:T(8,128)(2,1)} %fusion.39) | data formatting | bytes 16777216 | tf_op jit(solution)/shard_map/convert_element_type | solution.py:116
  627.0 218.8 %all_to_all.36 = bf16[512,32,2,128]{3,2,1,0:T(2,128)(2,1)} all-to-all(bf16[512,32,2,128]{3,2,1,0:T(2,128)(2,1)} %copy.45), channel_id=1, replica_groups=mesh['pen'=16,'coil'=2] {'pen'}, dimensions={0} | all-to-all | bytes 16777216 | tf_op jit(solution)/shard_map/all_to_all | solution.py:118
  863.8 14.8 %fusion.65 = f32[32,128,512,2,1]{2,1,4,3,0:T(8,128)} fusion(bf16[32,512,2,128,1]{3,1,2,4,0:T(8,128)(2,1)} %bitcast.157, f32[512,1,512,2]{2,0,3,1:T(8,128)S(1)} %copy-done.7, f32[512,1,512,2]{2,0,3,1:T(8,128)S(1)} %copy-done.5), kind=kOutput, calls=%fused_computation.99 | convolution fusion | flops 8594128896 | bytes 29360128 | tf_op jit(solution)/shard_map/kpxr,yxrz->ykpz/dot_general | solution.py:32
  878.6 19.0 %fusion.3 = f32[32,512,2,128]{1,3,2,0:T(8,128)} fusion(f32[32,128,512,2,1]{2,1,4,3,0:T(8,128)} %fusion.65, bf16[32,512,2,128,1]{3,1,2,4,0:T(8,128)(2,1)} %bitcast.158, f32[512,1,512,2]{2,0,3,1:T(8,128)} %get-tuple-element.17, f32[512,1,512,2]{2,0,3,1:T(8,128)S(1)} %copy-done.5), kind=kOutput, calls=%fused_computation.12 | convolution fusion | flops 8599371776 | bytes 46137344 | tf_op jit(solution)/shard_map/kpxr,yxrz->ykpz/dot_general | solution.py:33
  924.4 13.1 pad_dynamic-slice_fusion.5
  937.5 21.1 %fusion.15 = f32[32,257,2,127]{1,3,2,0:T(8,128)} fusion(s32[]{:T(128)S(6)} %select_n.65, s32[]{:T(128)S(6)} %add.172, f32[32,512,2,128]{1,3,2,0:T(8,128)} %copy.32), kind=kLoop, calls=%fused_computation.33 | loop fusion | flops 2088896 | bytes 25132808 | tf_op jit(solution)/shard_map/sub | solution.py:52
  958.7 23.7 %add_reduce_fusion = f32[32,257,128]{1,2,0:T(8,128)} fusion(f32[32,257,2,127]{1,3,2,0:T(8,128)} %fusion.15, f32[257]{0:T(512)S(1)} %get-tuple-element.21, s32[]{:T(128)S(6)} %select_n.65, f32[32,512,2,128]{1,3,2,0:T(8,128)} %copy.32, s32[]{:T(128)S(6)} %add.171, f32[32]{0:T(128)S(1)} %get-tuple-element.22, f32[1,258,2,128]{1,3,2,0:T(8,128)S(1)} %collective-permute-done, ...), kind=kLoop, calls=%fused_computation.40 | loop fusion | flops 22106112 | bytes 38062988 | tf_op jit(solution)/shard_map/reduce_sum | solution.py:55
  986.8 39.5 %divide_multiply_fusion.2 = (f32[32,257,2,128]{1,3,2,0:T(8,128)}, f32[32,257,2,128]{1,3,2,0:T(8,128)}, f32[32,257,2,128]{1,3,2,0:T(8,128)}) fusion(f32[32,257]{1,0:T(8,128)S(1)} %and_convert_fusion, f32[32,257,128]{1,2,0:T(8,128)S(1)} %add_sqrt_fusion, f32[32]{0:T(128)S(1)} %get-tuple-element.22, s32[]{:T(128)S(6)} %select_n.65, ...), kind=kLoop, calls=%fused_computation.39 | loop fusion | flops 23158784 | bytes 63360012 | tf_op jit(solution)/shard_map/mul | solution.py:60
  1050.2 250.9 %all-reduce.5.cloned.1.call-done = f32[32,512,2,128]{1,3,2,0:T(8,128)} async-done(((f32[32,512,2,128]{1,3,2,0:T(8,128)}), f32[32,512,2,128]{1,3,2,0:T(8,128)}) %all-reduce.5.cloned.1.call-update) | async-done | bytes 16777232 | tf_op jit(solution)/shard_map/psum | solution.py:126
  1301.1 28.7 %fusion.30 = f32[32,256,2,128]{1,3,2,0:T(8,128)} fusion(f32[32,257,2,128]{1,3,2,0:T(8,128)} %get-tuple-element.15, f32[32,257,2,128]{1,3,2,0:T(8,128)} %get-tuple-element.12, f32[32,257,2,128]{1,3,2,0:T(8,128)} %get-tuple-element.11, f32[31,257,2,128]{1,3,2,0:T(8,128)} %slice.90, f32[1,257,2,128]{1,3,2,0:T(8,128)S(1)} %collective-permute-done.1, ...), kind=kLoop, calls=%fused_computation.50 | loop fusion | flops 16777216 | bytes 67076100 | tf_op jit(solution)/shard_map/add | solution.py:142
  1329.8 13.1 copy.51
  (57 shorter events, 156.1 us)
Async XLA Ops:
  99.3 10.2 copy-start.1
  99.3 10.2 copy-start.2
  109.4 3.3 copy-start.3
  109.4 4.4 copy-start.4
  112.6 1.9 copy-start.8
  112.6 2.6 copy-start.10
  165.4 158.0 %all-to-all-start = ((bf16[32,512,2,128]{3,2,0,1:T(2,128)(2,1)}), bf16[32,512,2,128]{3,2,0,1:T(2,128)(2,1)}, u32[]{:S(2)}, u32[]{:S(2)}) async-start(bf16[32,512,2,128]{3,2,0,1:T(2,128)(2,1)} %copy.35), calls=%async_computation | async-start | bytes 16777216 | tf_op jit(solution)/shard_map/all_to_all | solution.py:91
  172.9 1128.3 %all-reduce.5.cloned.1.call-start = ((), (), s32[]{:S(2)}) async-start(), calls=%async_computation.2 | async-start | bytes 33554432 | tf_op jit(solution)/shard_map/psum | solution.py:126
  172.9 45.1 %copy-start.12 = (s32[256]{0:T(256)S(1)}, s32[256]{0:T(256)}, u32[]{:S(2)}) copy-start(s32[256]{0:T(256)} %param.9) | copy-start | bytes 3076
  349.2 14.0 %copy-start.9 = (f32[512,1,512,2]{2,0,3,1:T(8,128)S(1)}, f32[512,1,512,2]{2,0,3,1:T(8,128)}, u32[]{:S(2)}) copy-start(f32[512,1,512,2]{2,0,3,1:T(8,128)} %copy-done.8) | copy-start | bytes 6291460
  363.2 16.4 %copy-start.11 = (f32[512,1,512,2]{2,0,3,1:T(8,128)S(1)}, f32[512,1,512,2]{2,0,3,1:T(8,128)}, u32[]{:S(2)}) copy-start(f32[512,1,512,2]{2,0,3,1:T(8,128)} %copy-done.10) | copy-start | bytes 6291460
  558.8 13.2 copy-start.5
  572.1 16.8 %copy-start.6 = (f32[512,1,512,2]{2,0,3,1:T(8,128)S(1)}, f32[512,1,512,2]{2,0,3,1:T(8,128)}, u32[]{:S(2)}) copy-start(f32[512,1,512,2]{2,0,3,1:T(8,128)} %get-tuple-element.17) | copy-start | bytes 6291460
  854.7 9.1 copy-start.7
  878.6 19.0 %copy-start = (bf16[1,32,512,1,128]{2,4,1,3,0:T(8,128)(2,1)S(1)}, bf16[1,32,512,1,128]{2,4,1,3,0:T(8,128)(2,1)}, u32[]{:S(2)}) copy-start(bf16[1,32,512,1,128]{2,4,1,3,0:T(8,128)(2,1)} %copy.75) | copy-start | bytes 12582916
  923.1 35.6 %collective-permute-start = (f32[1,258,2,128]{1,3,2,0:T(8,128)S(1)}, f32[1,258,2,128]{1,3,2,0:T(8,128)S(1)}, u32[]{:S(2)}, u32[]{:S(2)}) collective-permute-start(f32[1,258,2,128]{1,3,2,0:T(8,128)S(1)} %pad_dynamic-slice_fusion.4), channel_id=1, source_target_pairs={{2,0},{4,2},{6,4},{8,6},{10,8},{12,10},{14,12},{16,14},{18,16},{20... | collective-permute-start | bytes 792584 | tf_op jit(solution)/shard_map/ppermute | solution.py:16
  1027.3 23.0 %collective-permute-start.1 = (f32[1,257,2,128]{1,3,2,0:T(8,128)S(1)}, f32[1,257,2,128]{1,3,2,0:T(8,128)S(1)}, u32[]{:S(2)}, u32[]{:S(2)}) collective-permute-start(f32[1,257,2,128]{1,3,2,0:T(8,128)S(1)} %slice.89), channel_id=1, source_target_pairs={{0,2},{2,4},{4,6},{6,8},{8,10},{10,12},{12,14},{14,16},{16,18},{18... | collective-permute-start | bytes 789512 | tf_op jit(solution)/shard_map/ppermute | solution.py:16
Sparse Core Ops, SparseCore 0:
  922.0 379.0 all-reduce.4
where the time goes:
time: 1360 us; the launch traced here: 1350 us
  local copies, waits for them, and re-layouts  393 us (29%)
  waiting for transfers between devices  356 us (26%)
  blocking collectives  219 us (16%)
  matrix products  189 us (14%)
  other arithmetic  169 us (12%)
  between operations  14.1 us (1%)
    psum x1, waiting for transfers between devices, on_device(): summed = lax.psum(coil_term, 'coil')  251 us
    all_to_all x1, blocking collectives, on_device(): lax.all_to_all(back_rows, 'pen', split_axis=0, concat_axis=1, tiled=True)  219 us
    all_to_all x1, waiting for transfers between devices, on_device(): lax.all_to_all(rows_spectrum, 'pen', split_axis=1, concat_axis=0, tiled=T...  105 us
    unnamed x29, local copies, waits for them, and re-layouts  64.2 us
    convert_element_type x1, local copies, waits for them, and re-layouts, on_device(): measured = samples[0].reshape(predicted.shape).astype(jnp.float32)  45.1 us
    all_to_all x3, local copies, waits for them, and re-layouts, on_device(): lax.all_to_all(rows_spectrum, 'pen', split_axis=1, concat_axis=0, tiled=T...  39.8 us
    mul x1, other arithmetic, flux_fields(): diff_y / norm_den * inside  39.5 us
    dot_general x1, matrix products, on_device(): jnp.einsum('bst,bsc->btc', kernels, misfit, preferred_element_type=jnp.fl...  38.4 us
  transfers between devices with their start and end apart: 4, of which 2 were waited for; matrix products, arithmetic and copies ran while one was open for 13% of the time, Pallas kernels for 0%

commit v1 on v0

--- a/solution.py
+++ b/solution.py
@@ -123,7 +123,7 @@
         [map_real * back_real + map_imag * back_imag, map_real * back_imag - map_imag * back_real],
         2,
     )
-    summed = lax.psum(coil_term, "coil")
+    summed = jnp.sum(lax.all_gather(coil_term, "coil"), axis=0)
     data_gradient = lax.dynamic_slice_in_dim(summed, col_start, half_cols, 1)
     padded = jnp.pad(image_field, ((0, 0), (1, 1), (0, 0), (0, 0)))
     window = lax.dynamic_slice_in_dim(padded, col_start, half_cols + 2, 1)

time: 1360 us -> 1430 us (1.051)
  local copies, waits for them, and re-layouts: 393 us -> 428 us
  other arithmetic: 169 us -> 189 us
    all_gather x0 -> x1, waiting for transfers between devices: none -> 257 us  [on_device(): summed = jnp.sum(lax.all_gather(coil_term, 'coil'), axis=0)]
    psum x1 -> x0, waiting for transfers between devices: 251 us -> none  [on_device(): summed = lax.psum(coil_term, 'coil')]
    reduce_sum x0 -> x1, other arithmetic: none -> 19.1 us  [on_device(): summed = jnp.sum(lax.all_gather(coil_term, 'coil'), axis=0)]
    another operation x0 -> x1, local copies, waits for them, and re-layouts: none -> 17.4 us  [on_device(): jnp.stack([map_real * back_real + map_imag * back_imag, map_real * back_i...]
    unnamed x29 -> x30, local copies, waits for them, and re-layouts: 64.2 us -> 73.2 us
  transfers between devices with their start and end apart: 4 -> 4, of which waited for: 2 -> 2; matrix products, arithmetic and copies ran while one was open for 13% -> 15% of each run, Pallas kernels for 0% -> 0%
where the time goes in v1:
time: 1430 us; the launch traced here: 1410 us
  local copies, waits for them, and re-layouts  428 us (30%)
  waiting for transfers between devices  363 us (25%)
  blocking collectives  219 us (15%)
  other arithmetic  189 us (13%)
  matrix products  189 us (13%)
    all_gather x1, waiting for transfers between devices, on_device(): summed = jnp.sum(lax.all_gather(coil_term, 'coil'), axis=0)  257 us
    all_to_all x1, blocking collectives, on_device(): lax.all_to_all(back_rows, 'pen', split_axis=0, concat_axis=1, tiled=True)  219 us
    all_to_all x1, waiting for transfers between devices, on_device(): lax.all_to_all(rows_spectrum, 'pen', split_axis=1, concat_axis=0, tiled=T...  105 us
    unnamed x30, local copies, waits for them, and re-layouts  73.2 us
    convert_element_type x1, local copies, waits for them, and re-layouts, on_device(): measured = samples[0].reshape(predicted.shape).astype(jnp.float32)  45.1 us
    all_to_all x3, local copies, waits for them, and re-layouts, on_device(): lax.all_to_all(rows_spectrum, 'pen', split_axis=1, concat_axis=0, tiled=T...  39.8 us
    dot_general x1, matrix products, on_device(): jnp.einsum('bst,bsc->btc', kernels, misfit, preferred_element_type=jnp.fl...  38.3 us
    mul x1, other arithmetic, flux_fields(): diff_y / norm_den * inside  36.8 us
  transfers between devices with their start and end apart: 4, of which 2 were waited for; matrix products, arithmetic and copies ran while one was open for 15% of the time, Pallas kernels for 0%

profile of v1, /device:TPU:0, one launch (start us, length us, event | category | flops | bytes accessed | tf_op | source)
XLA Modules:
  0.0 1414.1 jit_solution(6243430475982261849)
XLA Ops:
  20.2 25.0 %copy.28 = f32[32,512,2,128]{1,3,2,0:T(8,128)} copy(f32[32,512,2,128]{3,2,1,0:T(2,128)} %param.5) | data formatting | bytes 33554432 | tf_op args[0]
  45.2 17.7 %fusion.90 = (bf16[1,32,512,1,128]{4,3,2,1,0:T(2,128)(2,1)}, bf16[1,32,512,1,128]{4,3,2,1,0:T(2,128)(2,1)}) fusion(bf16[1,32,512,2,128]{4,3,2,1,0:T(2,128)(2,1)} %param.6), kind=kLoop, calls=%fused_computation.128 | loop fusion | bytes 16777216 | tf_op jit(solution)/shard_map/slice | solution.py:76
  62.9 18.3 %copy.74 = bf16[1,32,512,1,128]{2,4,1,3,0:T(8,128)(2,1)} copy(bf16[1,32,512,1,128]{4,3,2,1,0:T(2,128)(2,1)} %get-tuple-element.13) | data formatting | bytes 8388608
  81.3 18.3 %copy.75 = bf16[1,32,512,1,128]{2,4,1,3,0:T(8,128)(2,1)} copy(bf16[1,32,512,1,128]{4,3,2,1,0:T(2,128)(2,1)} %get-tuple-element.14) | data formatting | bytes 8388608
  127.0 17.4 %fusion.37 = bf16[32,512,2,128]{1,3,2,0:T(8,128)(2,1)} fusion(bf16[32,512,1,128]{1,3,2,0:T(8,128)(2,1)} %copy-done.4, bf16[32,512,1,128]{1,3,2,0:T(8,128)(2,1)} %copy-done.3, f32[32,128,512,2,1]{2,1,4,3,0:T(8,128)} %fusion.36, f32[512,1,512,2]{2,0,3,1:T(8,128)} %copy-done.8, f32[512,1,512,2]{2,0,3,1:T(8,128)} %copy-done.10), kind=kOutput, calls=%fused_computation.63 | convolution fusion | flops 8620343296 | bytes 37748736 | tf_op jit(solution)/shard_map/kpxr,yxrz->ykpz/dot_general | solution.py:33
  144.4 21.3 %copy.31 = bf16[32,512,2,128]{3,2,0,1:T(2,128)(2,1)} copy(bf16[32,512,2,128]{1,3,2,0:T(8,128)(2,1)} %fusion.37) | data formatting | bytes 16777216 | tf_op jit(solution)/shard_map/convert_element_type | solution.py:89
  173.2 45.1 %copy.38 = f32[1,256,128,2,128]{2,4,3,1,0:T(8,128)} copy(bf16[1,256,128,2,128]{4,3,2,1,0:T(2,128)(2,1)} %param.7) | data formatting | bytes 50331648 | tf_op jit(solution)/shard_map/convert_element_type | solution.py:102
  218.3 105.4 %all-to-all-done = bf16[32,512,2,128]{3,2,0,1:T(2,128)(2,1)} async-done(((bf16[32,512,2,128]{3,2,0,1:T(2,128)(2,1)}), bf16[32,512,2,128]{3,2,0,1:T(2,128)(2,1)}, u32[]{:S(2)}, u32[]{:S(2)}) %all-to-all-start) | async-done | bytes 8388640 | tf_op jit(solution)/shard_map/all_to_all | solution.py:91
  323.7 16.5 %copy.32 = bf16[32,512,2,128]{3,1,2,0:T(8,128)(2,1)} copy(bf16[32,512,2,128]{3,2,0,1:T(2,128)(2,1)} %all-to-all-done) | data formatting | bytes 16777216 | tf_op jit(solution)/shard_map/all_to_all | solution.py:91
  349.5 14.0 copy.53
  363.5 16.4 %fusion.68 = f32[32,128,512,2,1]{2,1,4,3,0:T(8,128)} fusion(bf16[512,32,2,128,1]{0,3,2,4,1:T(8,128)(2,1)} %copy.53, f32[512,1,512,2]{2,0,3,1:T(8,128)S(1)} %copy-done.9, f32[512,1,512,2]{2,0,3,1:T(8,128)} %copy-done.10), kind=kOutput, calls=%fused_computation.100 | convolution fusion | flops 8594128896 | bytes 29360128 | tf_op jit(solution)/shard_map/kpyr,yxrz->kxpz/dot_general | solution.py:39
  379.9 17.1 %fusion.38 = bf16[512,32,2,128]{0,3,2,1:T(8,128)(2,1)} fusion(bf16[512,32,2,128,1]{0,3,2,4,1:T(8,128)(2,1)} %copy.53, f32[32,128,512,2,1]{2,1,4,3,0:T(8,128)} %fusion.68, f32[512,1,512,2]{2,0,3,1:T(8,128)S(1)} %copy-done.9, f32[512,1,512,2]{2,0,3,1:T(8,128)S(1)} %copy-done.11), kind=kOutput, calls=%fused_computation.64 | convolution fusion | flops 8603566080 | bytes 37748736 | tf_op jit(solution)/shard_map/kpyr,yxrz->kxpz/dot_general | solution.py:40
  409.5 13.3 copy.36
  436.0 38.3 %fusion.10 = f32[256,128,256]{1,2,0:T(8,128)} fusion(bf16[256,128,128]{2,1,0:T(8,128)(2,1)} %param.8, f32[256,128,256]{1,2,0:T(8,128)} %bitcast.152, bf16[256,128,256]{2,1,0:T(8,128)(2,1)} %gather_fusion, pred[256]{0:T(512)(128)(4,1)S(1)} %get-tuple-element.5), kind=kOutput, calls=%fused_computation.30 | convolution fusion | flops 4320133120 | bytes 92274944 | tf_op jit(solution)/shard_map/bst,bsc->btc/dot_general | solution.py:104
  474.3 33.4 %copy.39 = f32[256,128,256]{2,0,1:T(8,128)} copy(f32[256,128,256]{1,2,0:T(8,128)} %fusion.10) | data formatting | bytes 67108864 | tf_op jit(solution)/shard_map/bst,bsc->btc/dot_general | solution.py:104
  507.7 20.8 %convolution_convert_fusion = bf16[128,128,256]{2,0,1:T(8,128)(2,1)} fusion(f32[256,128,256]{2,0,1:T(8,128)} %copy.39, s32[256]{0:T(256)S(1)} %get-tuple-element.6), kind=kOutput, calls=%fused_computation.60 | convolution fusion | flops 12889128960 | bytes 41944064 | tf_op jit(solution)/shard_map/bl,btc->ltc/dot_general | solution.py:108
  541.1 18.0 %copy.40 = bf16[4,128,32,256]{1,0,3,2:T(4,128)(2,1)} copy(bf16[4,128,32,256]{3,0,2,1:T(4,128)(2,1)} %bitcast.157) | data formatting | bytes 16777216 | tf_op jit(solution)/shard_map/transpose | solution.py:113
  559.1 13.2 reshape.239
  572.3 16.8 %fusion.32 = f32[32,128,512,2,1]{2,1,4,3,0:T(8,128)} fusion(bf16[512,32,2,128,1]{0,3,2,1,4:T(8,128)(2,1)} %reshape.239, f32[512,1,512,2]{2,0,3,1:T(8,128)} %get-tuple-element.17, f32[512,1,512,2]{2,0,3,1:T(8,128)S(1)} %copy-done.5), kind=kOutput, calls=%fused_computation.57 | convolution fusion | flops 8594128896 | bytes 29360128 | tf_op jit(solution)/shard_map/kpyr,yxrz->kxpz/dot_general | solution.py:39
  589.1 16.9 %fusion.39 = bf16[512,32,2,128]{0,3,2,1:T(8,128)(2,1)} fusion(bf16[512,32,2,128,1]{0,3,2,1,4:T(8,128)(2,1)} %reshape.239, f32[32,128,512,2,1]{2,1,4,3,0:T(8,128)} %fusion.32, f32[512,1,512,2]{2,0,3,1:T(8,128)S(1)} %copy-done.6, f32[512,1,512,2]{2,0,3,1:T(8,128)S(1)} %copy-done.5), kind=kOutput, calls=%fused_computation.65 | convolution fusion | flops 8603566080 | bytes 37748736 | tf_op jit(solution)/shard_map/kpyr,yxrz->kxpz/dot_general | solution.py:40
  606.1 21.2 %copy.41 = bf16[512,32,2,128]{3,2,1,0:T(2,128)(2,1)} copy(bf16[512,32,2,128]{0,3,2,1:T(8,128)(2,1)} %fusion.39) | data formatting | bytes 16777216 | tf_op jit(solution)/shard_map/convert_element_type | solution.py:116
  627.3 218.8 %all_to_all.36 = bf16[512,32,2,128]{3,2,1,0:T(2,128)(2,1)} all-to-all(bf16[512,32,2,128]{3,2,1,0:T(2,128)(2,1)} %copy.41), channel_id=1, replica_groups=mesh['pen'=16,'coil'=2] {'pen'}, dimensions={0} | all-to-all | bytes 16777216 | tf_op jit(solution)/shard_map/all_to_all | solution.py:118
  864.0 14.8 %fusion.65 = f32[32,128,512,2,1]{2,1,4,3,0:T(8,128)} fusion(bf16[32,512,2,128,1]{3,1,2,4,0:T(8,128)(2,1)} %bitcast.159, f32[512,1,512,2]{2,0,3,1:T(8,128)S(1)} %copy-done.7, f32[512,1,512,2]{2,0,3,1:T(8,128)S(1)} %copy-done.5), kind=kOutput, calls=%fused_computation.99 | convolution fusion | flops 8594128896 | bytes 29360128 | tf_op jit(solution)/shard_map/kpxr,yxrz->ykpz/dot_general | solution.py:32
  878.8 19.0 %fusion.3 = f32[32,512,2,128]{1,3,2,0:T(8,128)} fusion(f32[32,128,512,2,1]{2,1,4,3,0:T(8,128)} %fusion.65, bf16[32,512,2,128,1]{3,1,2,4,0:T(8,128)(2,1)} %bitcast.160, f32[512,1,512,2]{2,0,3,1:T(8,128)} %get-tuple-element.17, f32[512,1,512,2]{2,0,3,1:T(8,128)S(1)} %copy-done.5), kind=kOutput, calls=%fused_computation.12 | convolution fusion | flops 8599371776 | bytes 46137344 | tf_op jit(solution)/shard_map/kpxr,yxrz->ykpz/dot_general | solution.py:33
  922.0 17.4 %copy.46 = f32[32,512,2,128]{3,1,2,0:T(8,128)} copy(f32[32,512,2,128]{1,3,2,0:T(8,128)} %pad_maximum_fusion) | data formatting | bytes 33554432 | tf_op jit(solution)/shard_map/stack | solution.py:122
  942.0 14.9 %pad_dynamic-slice_fusion.5 = f32[32,258,2,128]{1,3,2,0:T(8,128)} fusion(s32[]{:T(128)S(6)} %select_n.65, f32[32,512,2,128]{1,3,2,0:T(8,128)} %copy.28), kind=kLoop, calls=%fused_computation.8 | loop fusion | bytes 25231364 | tf_op jit(solution)/shard_map/dynamic_slice | solution.py:129
  956.9 23.7 %fusion.15 = f32[32,257,2,127]{1,3,2,0:T(8,128)} fusion(s32[]{:T(128)S(6)} %select_n.65, s32[]{:T(128)S(6)} %add.170, f32[32,512,2,128]{1,3,2,0:T(8,128)} %copy.28), kind=kLoop, calls=%fused_computation.33 | loop fusion | flops 2088896 | bytes 25132808 | tf_op jit(solution)/shard_map/sub | solution.py:52
  980.7 25.5 %add_reduce_fusion = f32[32,257,128]{1,2,0:T(8,128)} fusion(f32[32,257,2,127]{1,3,2,0:T(8,128)} %fusion.15, f32[257]{0:T(512)S(1)} %get-tuple-element.25, s32[]{:T(128)S(6)} %select_n.65, f32[32,512,2,128]{1,3,2,0:T(8,128)} %copy.28, s32[]{:T(128)S(6)} %add.169, f32[32]{0:T(128)S(1)} %get-tuple-element.26, f32[1,258,2,128]{1,3,2,0:T(8,128)S(1)} %collective-permute-done, ...), kind=kLoop, calls=%fused_computation.40 | loop fusion | flops 22106112 | bytes 38062988 | tf_op jit(solution)/shard_map/reduce_sum | solution.py:55
  1010.7 36.8 %divide_multiply_fusion.2 = (f32[32,257,2,128]{1,3,2,0:T(8,128)}, f32[32,257,2,128]{1,3,2,0:T(8,128)}, f32[32,257,2,128]{1,3,2,0:T(8,128)}) fusion(f32[32,257]{1,0:T(8,128)S(1)} %and_convert_fusion, f32[32,257,128]{1,2,0:T(8,128)S(1)} %add_sqrt_fusion, f32[32]{0:T(128)S(1)} %get-tuple-element.26, s32[]{:T(128)S(6)} %select_n.65, ...), kind=kLoop, calls=%fused_computation.39 | loop fusion | flops 23158784 | bytes 63360012 | tf_op jit(solution)/shard_map/mul | solution.py:60
  1072.1 257.1 %all-gather.3.cloned.1.call-done = f32[64,512,2,128]{3,1,2,0:T(8,128)} async-done(((f32[32,512,2,128]{3,1,2,0:T(8,128)}), f32[64,512,2,128]{3,1,2,0:T(8,128)}) %all-gather.3.cloned.1.call-update) | async-done | bytes 33554448 | tf_op jit(solution)/shard_map/all_gather | solution.py:126
  1329.3 19.1 %reduce_sum.18 = f32[32,512,2,128]{3,1,2,0:T(8,128)} reduce(f32[2,32,512,2,128]{4,2,3,1,0:T(8,128)} %bitcast.154, f32[]{:T(128)} %constant.68.clone.1), dimensions={0}, to_apply=%region_0.1 | reduce | flops 4194304 | bytes 50331652 | tf_op jit(solution)/shard_map/reduce_sum | solution.py:126
  1365.1 28.6 %fusion.30 = f32[32,256,2,128]{1,3,2,0:T(8,128)} fusion(f32[32,256,2,128]{1,3,2,0:T(8,128)} %copy.76, f32[32,257,2,128]{1,3,2,0:T(8,128)} %get-tuple-element.15, f32[32,257,2,128]{1,3,2,0:T(8,128)} %get-tuple-element.12, f32[32,257,2,128]{1,3,2,0:T(8,128)} %get-tuple-element.11, f32[31,257,2,128]{1,3,2,0:T(8,128)} %slice.90, ...), kind=kLoop, calls=%fused_computation.50 | loop fusion | flops 16777216 | bytes 67076096 | tf_op jit(solution)/shard_map/add | solution.py:142
  (61 shorter events, 199.7 us)
Async XLA Ops:
  99.6 10.2 copy-start.1
  99.6 10.2 copy-start.2
  109.7 3.3 copy-start.3
  109.7 4.4 copy-start.4
  112.9 1.9 copy-start.8
  112.9 2.6 copy-start.10
  165.7 158.0 %all-to-all-start = ((bf16[32,512,2,128]{3,2,0,1:T(2,128)(2,1)}), bf16[32,512,2,128]{3,2,0,1:T(2,128)(2,1)}, u32[]{:S(2)}, u32[]{:S(2)}) async-start(bf16[32,512,2,128]{3,2,0,1:T(2,128)(2,1)} %copy.31), calls=%async_computation | async-start | bytes 16777216 | tf_op jit(solution)/shard_map/all_to_all | solution.py:91
  173.1 1156.1 %all-gather.3.cloned.1.call-start = ((), (), s32[]{:S(2)}) async-start(), calls=%async_computation.2 | async-start | bytes 50331648 | tf_op jit(solution)/shard_map/all_gather | solution.py:126
  173.2 45.1 %copy-start.12 = (s32[256]{0:T(256)S(1)}, s32[256]{0:T(256)}, u32[]{:S(2)}) copy-start(s32[256]{0:T(256)} %param.9) | copy-start | bytes 3076
  349.5 14.0 copy-start.9
  363.5 16.4 %copy-start.11 = (f32[512,1,512,2]{2,0,3,1:T(8,128)S(1)}, f32[512,1,512,2]{2,0,3,1:T(8,128)}, u32[]{:S(2)}) copy-start(f32[512,1,512,2]{2,0,3,1:T(8,128)} %copy-done.10) | copy-start | bytes 6291460
  559.1 13.2 copy-start.5
  572.3 16.8 %copy-start.6 = (f32[512,1,512,2]{2,0,3,1:T(8,128)S(1)}, f32[512,1,512,2]{2,0,3,1:T(8,128)}, u32[]{:S(2)}) copy-start(f32[512,1,512,2]{2,0,3,1:T(8,128)} %get-tuple-element.17) | copy-start | bytes 6291460
  855.0 9.1 copy-start.7
  878.8 19.0 %copy-start = (bf16[1,32,512,1,128]{2,4,1,3,0:T(8,128)(2,1)S(1)}, bf16[1,32,512,1,128]{2,4,1,3,0:T(8,128)(2,1)}, u32[]{:S(2)}) copy-start(bf16[1,32,512,1,128]{2,4,1,3,0:T(8,128)(2,1)} %copy.74) | copy-start | bytes 12582916
  940.7 40.0 %collective-permute-start = (f32[1,258,2,128]{1,3,2,0:T(8,128)S(1)}, f32[1,258,2,128]{1,3,2,0:T(8,128)S(1)}, u32[]{:S(2)}, u32[]{:S(2)}) collective-permute-start(f32[1,258,2,128]{1,3,2,0:T(8,128)S(1)} %pad_dynamic-slice_fusion.4), channel_id=1, source_target_pairs={{2,0},{4,2},{6,4},{8,6},{10,8},{12,10},{14,12},{16,14},{18,16},{20... | collective-permute-start | bytes 792584 | tf_op jit(solution)/shard_map/ppermute | solution.py:16
  1068.9 296.2 %collective-permute-start.1 = (f32[1,257,2,128]{1,3,2,0:T(8,128)S(1)}, f32[1,257,2,128]{1,3,2,0:T(8,128)S(1)}, u32[]{:S(2)}, u32[]{:S(2)}) collective-permute-start(f32[1,257,2,128]{1,3,2,0:T(8,128)S(1)} %slice.89), channel_id=1, source_target_pairs={{0,2},{2,4},{4,6},{6,8},{8,10},{10,12},{12,14},{14,16},{16,18},{18... | collective-permute-start | bytes 789512 | tf_op jit(solution)/shard_map/ppermute | solution.py:16
Sparse Core Ops, SparseCore 0:
  939.6 389.6 all-gather.2
